TPU v7x, 32 devices: a whole 2x2x4 slice. The times are simulated.
32 devices in a mesh: row: 4 (over x, core), col: 2 (over y), depth: 4 (over z).
Axes of the slice: x: 2, y: 2, z: 4, core: 2. Of those that a mesh axis runs over, the one named last changes fastest.
Arguments:
- tokens: bfloat16 [64, 6144], P(('col', 'depth'), 'row'), may hold values from -6 to 6
- first_weight: bfloat16 [6144, 24576], P('row', ('col', 'depth')), may hold values from -0.078125 to 0.078125
- first_tangent: bfloat16 [6144, 24576], P('row', ('col', 'depth')), may hold values from -0.078125 to 0.078125
- second_weight: bfloat16 [24576, 6144], P(('col', 'depth'), 'row'), may hold values from -0.0390625 to 0.0390625
- second_tangent: bfloat16 [24576, 6144], P(('col', 'depth'), 'row'), may hold values from -0.0390625 to 0.0390625
Outputs:
- grad_first: float32 [6144, 24576], P('row', ('col', 'depth'))
- grad_second: float32 [24576, 6144], P(('col', 'depth'), 'row')
All inputs are finite; a program needn't handle non-finite values.
Results may differ from a plain program's by a relative error of at most 0.0047.
Values may be sent and summed in bfloat16 or wider, within the bound.
A program may use at most 192 MiB of HBM per device.

v0:
```python
import functools
import math

import jax
import jax.numpy as jnp
from jax import lax
from jax.experimental import pallas as pl
from jax.experimental.pallas import tpu as pltpu
from jax.sharding import PartitionSpec as P

CORES = 2
LANES = 128
F32 = jnp.float32
BF16 = jnp.bfloat16


def pieces(extent, most):
    return max(n for n in range(1, most + 1) if extent % (n * LANES) == 0)


def gelu_parts(hidden, hidden_tan):
    inner = 0.7978845608 * (hidden + 0.044715 * hidden * hidden * hidden)
    tval = jnp.tanh(inner)
    active = 0.5 * hidden * (1.0 + tval)
    slopes = 0.5 * (1.0 + tval) + 0.5 * hidden * (1.0 - tval * tval) * 0.7978845608 * (
        1.0 + 3.0 * 0.044715 * hidden * hidden
    )
    return active, slopes * hidden_tan, slopes


def block_kernel(
    sizes,
    tok_ref, fw_ref, ft_ref, sw_ref, st_ref,
    tok_out, act_out, tan_out, back_out,
    w1, w2, tokg, tok2d, hbuf, psend, precv, xsend, xrecv, acts, slopes,
    acc, rsend, rrecv, outg, bsend, brecv, bxsend, bxrecv, back,
    wsem, tok_s, tok_r, ps, pr, xs, xr, as_, ar, rs, rr, gs, gr, bps, bpr, bxs, bxr, bas, bar_,
):
    chips, ncol, ndepth, nf, no = sizes
    group = ncol * ndepth
    tl, dl = tok_ref.shape
    total = group * tl
    half = total // CORES
    cw = w1.shape[-1]
    dn = dl // no

    row = lax.axis_index("row")
    core = lax.rem(row, CORES)
    chip = lax.div(row, CORES)
    mate = {"row": chip * CORES + (1 - core)}
    across = [{"row": lax.rem(chip + o, chips) * CORES + core} for o in range(1, chips)]
    me = lax.axis_index("col") * ndepth + lax.axis_index("depth")
    ranks = [lax.rem(me + o, group) for o in range(1, group)]
    peers = [{"col": lax.div(r, ndepth), "depth": lax.rem(r, ndepth)} for r in ranks]
    mine = pl.ds(pl.multiple_of(core * half, half), half)
    other = pl.ds(pl.multiple_of((1 - core) * half, half), half)

    loads = {}
    for i, ref in enumerate((fw_ref, ft_ref)):
        for k in range(nf):
            loads[i, k] = pltpu.make_async_copy(
                ref.at[:, pl.ds(k * cw, cw)], w1.at[i, k], wsem.at[i, k]
            )
    for i, ref in enumerate((sw_ref, st_ref)):
        for k in range(nf):
            loads[2 + i, k] = pltpu.make_async_copy(
                ref.at[pl.ds(k * cw, cw), :], w2.at[i, k], wsem.at[2 + i, k]
            )
    for pair in (0, 2):
        for k in range(nf):
            loads[pair, k].start()
            loads[pair + 1, k].start()

    sent = []

    def send(src, dst, ssem, rsem, device):
        copy = pltpu.make_async_remote_copy(
            src_ref=src, dst_ref=dst, send_sem=ssem, recv_sem=rsem,
            device_id=device, device_id_type=pl.DeviceIdType.MESH,
        )
        copy.start()
        sent.append(copy)
        return copy

    barrier = pltpu.get_barrier_semaphore()
    everyone = [mate] + across + peers
    for device in everyone:
        pl.semaphore_signal(
            barrier, inc=1, device_id=device, device_id_type=pl.DeviceIdType.MESH
        )
    pl.semaphore_wait(barrier, len(everyone))

    arrivals = [
        send(tok_ref, tokg.at[me], tok_s.at[o], tok_r.at[o], device)
        for o, device in enumerate(peers)
    ]
    tokg[me] = tok_ref[...]
    for copy in arrivals:
        copy.wait_recv()
    tok2d[...] = tokg[...].astype(F32).reshape(total, dl).astype(BF16)
    tok_out[...] = tok2d[...]

    cols = [pl.ds(k * cw, cw) for k in range(nf)]
    to_mate, to_chips, halves = {}, {}, {}

    def first(k):
        for i in range(2):
            loads[i, k].wait()
            hbuf[i, :, cols[k]] = jnp.dot(tok2d[...], w1[i, k], preferred_element_type=F32)
            psend[k, i] = hbuf[i, other, cols[k]]
        to_mate[k] = send(psend.at[k], precv.at[k], ps.at[k], pr.at[k], mate)

    def chip_sum(k):
        to_mate[k].wait_recv()
        for i in range(2):
            both = hbuf[i, mine, cols[k]] + precv[k, i]
            hbuf[i, mine, cols[k]] = both
            xsend[k, i] = both.astype(BF16)
        to_chips[k] = [
            send(xsend.at[k], xrecv.at[o, k], xs.at[o, k], xr.at[o, k], device)
            for o, device in enumerate(across)
        ]

    def activate(k):
        hidden, hidden_tan = hbuf[0, mine, cols[k]], hbuf[1, mine, cols[k]]
        for o, copy in enumerate(to_chips[k]):
            copy.wait_recv()
            hidden = hidden + xrecv[o, k, 0].astype(F32)
            hidden_tan = hidden_tan + xrecv[o, k, 1].astype(F32)
        active, active_tan, slope = gelu_parts(hidden, hidden_tan)
        acts[k, 0, mine, :] = active_tan.astype(BF16)
        acts[k, 1, mine, :] = active.astype(BF16)
        slopes[:, cols[k]] = slope
        part = acts.at[k, :, mine, :]
        halves[k] = send(part, part, as_.at[k], ar.at[k], mate)

    scatter, gather = {}, {}

    def second(k):
        halves[k].wait_recv()
        for i in range(2):
            loads[2 + i, k].wait()
        for n in range(no):
            part = pl.ds(n * dn, dn)
            term = jnp.dot(acts[k, 0], w2[0, k, :, part], preferred_element_type=F32)
            term += jnp.dot(acts[k, 1], w2[1, k, :, part], preferred_element_type=F32)
            if k > 0:
                term += acc[n]
            acc[n] = term
            if k == nf - 1:
                rsend[n] = term.reshape(group, tl, dn).astype(BF16)
                scatter[n] = [
                    send(rsend.at[n, r], rrecv.at[n, o], rs.at[n, o], rr.at[n, o], device)
                    for o, (r, device) in enumerate(zip(ranks, peers))
                ]

    for t in range(nf + 6):
        for lag, stage in ((0, first), (2, chip_sum), (4, activate), (6, second)):
            if 0 <= t - lag < nf:
                stage(t - lag)

    for n in range(no):
        value = acc[n, pl.ds(pl.multiple_of(me * tl, tl), tl), :]
        for o, copy in enumerate(scatter[n]):
            copy.wait_recv()
            value += rrecv[n, o].astype(F32)
        outg[n, me] = value.astype(BF16)
        gather[n] = [
            send(outg.at[n, me], outg.at[n, me], gs.at[n, o], gr.at[n, o], device)
            for o, device in enumerate(peers)
        ]

    to_mate, to_chips, halves = {}, {}, {}

    def back_chip_sum(k):
        to_mate[k].wait_recv()
        both = hbuf[0, mine, cols[k]] + brecv[k]
        hbuf[0, mine, cols[k]] = both
        bxsend[k] = both.astype(BF16)
        to_chips[k] = [
            send(bxsend.at[k], bxrecv.at[o, k], bxs.at[o, k], bxr.at[o, k], device)
            for o, device in enumerate(across)
        ]

    def back_finish(k):
        value = hbuf[0, mine, cols[k]]
        for o, copy in enumerate(to_chips[k]):
            copy.wait_recv()
            value += bxrecv[o, k].astype(F32)
        back[k, mine, :] = (value * slopes[:, cols[k]]).astype(BF16)
        part = back.at[k, mine, :]
        halves[k] = send(part, part, bas.at[k], bar_.at[k], mate)

    for n in range(no):
        for copy in gather[n]:
            copy.wait_recv()
        part = pl.ds(n * dn, dn)
        tan_out[:, part] = outg[n].astype(F32).reshape(total, dn).astype(BF16)
        for k in range(nf):
            term = lax.dot_general(
                tan_out[:, part], w2[0, k, :, part], (((1,), (1,)), ((), ())),
                preferred_element_type=F32,
            )
            if n > 0:
                term += hbuf[0, :, cols[k]]
            hbuf[0, :, cols[k]] = term
            if n == no - 1:
                bsend[k] = hbuf[0, other, cols[k]]
                to_mate[k] = send(bsend.at[k], brecv.at[k], bps.at[k], bpr.at[k], mate)
                if k >= 2:
                    back_chip_sum(k - 2)
                if k >= 5:
                    back_finish(k - 5)
    for k in range(max(0, nf - 2), nf):
        back_chip_sum(k)
    for k in range(max(0, nf - 5), nf):
        back_finish(k)
    for k in range(nf):
        act_out[k] = acts[k, 1]
    for k in range(nf):
        halves[k].wait_recv()
        back_out[k] = back[k]
    for copy in sent:
        copy.wait_send()


def grads_kernel(factor, tok_ref, act_ref, tan_ref, back_ref, first_ref, second_ref):
    lhs_rows = (((0,), (0,)), ((), ()))
    second_ref[...] = (
        lax.dot_general(act_ref[0], tan_ref[...], lhs_rows, preferred_element_type=F32) * factor
    )
    first_ref[...] = (
        lax.dot_general(tok_ref[...], back_ref[0], lhs_rows, preferred_element_type=F32) * factor
    )


def on_device(axes, tokens, first_weight, first_tangent, second_weight, second_tangent):
    tl, dl = tokens.shape
    fl = first_weight.shape[1]
    ncol, ndepth, chips = axes["col"], axes["depth"], axes["row"] // CORES
    group = ncol * ndepth
    total, half = group * tl, group * tl // CORES
    nf, no = pieces(fl, 6), pieces(dl, 3)
    cw, dn = fl // nf, dl // no
    far = max(chips - 1, 1)
    dma = pltpu.SemaphoreType.DMA
    whole = pl.BlockSpec(memory_space=pltpu.VMEM)
    hbm = pl.BlockSpec(memory_space=pl.ANY)
    gathered, active, out_tan, back_hidden = pl.pallas_call(
        functools.partial(block_kernel, (chips, ncol, ndepth, nf, no)),
        name="block",
        out_shape=(
            jax.ShapeDtypeStruct((total, dl), BF16),
            jax.ShapeDtypeStruct((nf, total, cw), BF16),
            jax.ShapeDtypeStruct((total, dl), BF16),
            jax.ShapeDtypeStruct((nf, total, cw), BF16),
        ),
        in_specs=[whole, hbm, hbm, hbm, hbm],
        out_specs=(whole,) * 4,
        scratch_shapes=[
            pltpu.VMEM((2, nf, dl, cw), BF16),
            pltpu.VMEM((2, nf, cw, dl), BF16),
            pltpu.VMEM((group, tl, dl), BF16),
            pltpu.VMEM((total, dl), BF16),
            pltpu.VMEM((2, total, fl), F32),
            pltpu.VMEM((nf, 2, half, cw), F32),
            pltpu.VMEM((nf, 2, half, cw), F32),
            pltpu.VMEM((nf, 2, half, cw), BF16),
            pltpu.VMEM((far, nf, 2, half, cw), BF16),
            pltpu.VMEM((nf, 2, total, cw), BF16),
            pltpu.VMEM((half, fl), F32),
            pltpu.VMEM((no, total, dn), F32),
            pltpu.VMEM((no, group, tl, dn), BF16),
            pltpu.VMEM((no, group - 1, tl, dn), BF16),
            pltpu.VMEM((no, group, tl, dn), BF16),
            pltpu.VMEM((nf, half, cw), F32),
            pltpu.VMEM((nf, half, cw), F32),
            pltpu.VMEM((nf, half, cw), BF16),
            pltpu.VMEM((far, nf, half, cw), BF16),
            pltpu.VMEM((nf, total, cw), BF16),
            dma((4, nf)),
            dma((group - 1,)), dma((group - 1,)),
            dma((nf,)), dma((nf,)),
            dma((far, nf)), dma((far, nf)),
            dma((nf,)), dma((nf,)),
            dma((no, group - 1)), dma((no, group - 1)),
            dma((no, group - 1)), dma((no, group - 1)),
            dma((nf,)), dma((nf,)),
            dma((far, nf)), dma((far, nf)),
            dma((nf,)), dma((nf,)),
        ],
        compiler_params=pltpu.CompilerParams(
            collective_id=0, has_side_effects=True, vmem_limit_bytes=62 * 1024 * 1024
        ),
    )(tokens, first_weight, first_tangent, second_weight, second_tangent)

    return pl.pallas_call(
        functools.partial(grads_kernel, 1.0 / math.sqrt(total)),
        name="grads",
        grid=(nf,),
        out_shape=(
            jax.ShapeDtypeStruct((dl, fl), F32),
            jax.ShapeDtypeStruct((fl, dl), F32),
        ),
        in_specs=[
            pl.BlockSpec((total, dl), lambda k: (0, 0)),
            pl.BlockSpec((1, total, cw), lambda k: (k, 0, 0)),
            pl.BlockSpec((total, dl), lambda k: (0, 0)),
            pl.BlockSpec((1, total, cw), lambda k: (k, 0, 0)),
        ],
        out_specs=(
            pl.BlockSpec((dl, cw), lambda k: (0, k)),
            pl.BlockSpec((cw, dl), lambda k: (k, 0)),
        ),
    )(gathered, active, out_tan, back_hidden)


def solution(mesh):
    return jax.shard_map(
        functools.partial(on_device, dict(mesh.shape)),
        mesh=mesh,
        in_specs=(
            P(("col", "depth"), "row"),
            P("row", ("col", "depth")),
            P("row", ("col", "depth")),
            P(("col", "depth"), "row"),
            P(("col", "depth"), "row"),
        ),
        out_specs=(P("row", ("col", "depth")), P(("col", "depth"), "row")),
        check_vma=False,
    )
```

profile of v0, /device:TPU:0, one launch (start us, length us, event | category | flops | bytes accessed | tf_op | source)
XLA Modules:
  0.0 64.5 jit_solution(4488699409898595669)
XLA Ops:
  0.6 49.9 %block.1 = (bf16[64,1536]{1,0:T(8,128)(2,1)}, bf16[6,64,512]{2,1,0:T(8,128)(2,1)}, bf16[64,1536]{1,0:T(8,128)(2,1)}, bf16[6,64,512]{2,1,0:T(8,128)(2,1)}) custom-call(bf16[8,1536]{1,0:T(8,128)(2,1)} %tok_ref.1, bf16[1536,3072]{1,0:T(8,128)(2,1)} %fw_ref.1, bf16[1536,3072]{1,0:T(8,128)(2,1)} %ft_ref.1, bf16[3072,1536]{1,0:T(8,128)(2,1)} %sw_ref.1, ...), custom_call_target="tpu_custom_call" | custom-call | tf_op jit(solution)/shard_map/block/pallas_call | solution.py:249
  50.5 14.0 %grads.1 = (f32[1536,3072]{1,0:T(8,128)}, f32[3072,1536]{1,0:T(8,128)}) custom-call(bf16[64,1536]{1,0:T(8,128)(2,1)} %get-tuple-element.6.tok_ref, bf16[6,64,512]{2,1,0:T(8,128)(2,1)} %get-tuple-element.7.act_ref, bf16[64,1536]{1,0:T(8,128)(2,1)} %get-tuple-element.8.tan_ref, bf16[6,64,512]{2,1,0:T(8,128)(2,1)} %get-tuple-element.9.back_ref), custom_call_target="tpu_custom_call" | custom-call | tf_op jit(solution)/shard_map/grads/pallas_call | solution.py:297
where the time goes:
time: 64.6 us; the launch traced here: 64.5 us
  Pallas kernels  63.8 us (99%)
    pallas_call x1, Pallas kernels, on_device(): pl.pallas_call(functools.partial(block_kernel, (chips, ncol, ndepth, nf,...  49.9 us
    pallas_call x1, Pallas kernels, on_device(): pl.pallas_call(functools.partial(grads_kernel, 1.0 / math.sqrt(total)), n...  14 us

commit v1 on v0

v1 whole, which is shorter than its diff:
```python
import functools
import math

import jax
import jax.numpy as jnp
from jax import lax
from jax.experimental import pallas as pl
from jax.experimental.pallas import tpu as pltpu
from jax.sharding import PartitionSpec as P

CORES = 2
LAG_CHIP, LAG_SECOND = 3, 2
VMEM_MIB, GRADS_MIB, GROUPS, STEPS = 52, 30, 3, 12
LANES = 128
F32 = jnp.float32
BF16 = jnp.bfloat16


def pieces(extent, most):
    return max(n for n in range(1, most + 1) if extent % (n * LANES) == 0)


def gelu_parts(hidden, hidden_tan):
    inner = 0.7978845608 * (hidden + 0.044715 * hidden * hidden * hidden)
    tval = jnp.tanh(inner)
    active = 0.5 * hidden * (1.0 + tval)
    slopes = 0.5 * (1.0 + tval) + 0.5 * hidden * (1.0 - tval * tval) * 0.7978845608 * (
        1.0 + 3.0 * 0.044715 * hidden * hidden
    )
    return active, slopes * hidden_tan, slopes


def block_kernel(
    sizes,
    tok_ref, fw_ref, ft_ref, sw_ref, st_ref,
    tok_out, act_out, tan2d, cross_out, sum_out, slopes,
    w1, w2, tokg, tok2d, hbuf, precv, xsend, xrecv, acts,
    acc, rsend, rrecv, outg, bbuf, brecv,
    wsem, own_s, tok_s, tok_r,
    ps, pr, xs, xr, as_, ar, rs, rr, gs, gr, bps, bpr,
):
    chips, ncol, ndepth, nw, nf, no = sizes
    group = ncol * ndepth
    tl, dl = tok_ref.shape
    total = group * tl
    half = total // CORES
    ww = w1.shape[-1]
    fl = nw * ww
    cw, dn = fl // nf, dl // no

    row = lax.axis_index("row")
    core = lax.rem(row, CORES)
    chip = lax.div(row, CORES)
    mate = {"row": chip * CORES + (1 - core)}
    across = [{"row": lax.rem(chip + o, chips) * CORES + core} for o in range(1, chips)]
    me = lax.axis_index("col") * ndepth + lax.axis_index("depth")
    ranks = [lax.rem(me + o, group) for o in range(1, group)]
    peers = [{"col": lax.div(r, ndepth), "depth": lax.rem(r, ndepth)} for r in ranks]
    mine = pl.ds(pl.multiple_of(core * half, half), half)
    other = pl.ds(pl.multiple_of((1 - core) * half, half), half)

    barrier = pltpu.get_barrier_semaphore()
    entry = [mate] + across + peers
    for device in entry:
        pl.semaphore_signal(
            barrier, inc=1, device_id=device, device_id_type=pl.DeviceIdType.MESH
        )

    own = pltpu.make_async_copy(tok_ref, tokg.at[me], own_s)
    own.start()
    loads = {}
    for i, ref in enumerate((fw_ref, ft_ref)):
        for k in range(nw):
            loads[i, k] = pltpu.make_async_copy(
                ref.at[:, pl.ds(k * ww, ww)], w1.at[i, k], wsem.at[i, k]
            )
    for i, ref in enumerate((sw_ref, st_ref)):
        for k in range(nw):
            loads[2 + i, k] = pltpu.make_async_copy(
                ref.at[pl.ds(k * ww, ww), :], w2.at[i, k], wsem.at[2 + i, k]
            )
    for pair in (0, 2):
        for k in range(nw):
            loads[pair, k].start()
            loads[pair + 1, k].start()
    loaded = set()

    def load(i, k):
        if (i, k) not in loaded:
            loaded.add((i, k))
            loads[i, k].wait()

    sent = []

    def send(src, dst, ssem, rsem, device):
        copy = pltpu.make_async_remote_copy(
            src_ref=src, dst_ref=dst, send_sem=ssem, recv_sem=rsem,
            device_id=device, device_id_type=pl.DeviceIdType.MESH,
        )
        copy.start()
        sent.append(copy)
        return copy

    own.wait()
    pl.semaphore_wait(barrier, len(entry))

    arrivals = [
        send(tokg.at[me], tokg.at[me], tok_s.at[o], tok_r.at[o], device)
        for o, device in enumerate(peers)
    ]
    for copy in arrivals:
        copy.wait_recv()
    tok2d[...] = tokg[...].astype(F32).reshape(total, dl).astype(BF16)

    tok_out[pl.ds(0, half), :] = tok2d[mine, :]
    tok_out[pl.ds(half, half), :] = tok2d[other, :]

    cols = [pl.ds(k * cw, cw) for k in range(nf)]
    to_mate, to_chips, halves = {}, {}, {}
    per = nf // nw

    for i in range(2):
        for k in range(nw):
            load(i, k)

    def first(k):
        for i in range(2):
            weight = w1[i, k // per, :, pl.ds((k % per) * cw, cw)]
            hbuf[i, :, cols[k]] = jnp.dot(tok2d[...], weight, preferred_element_type=F32)
        to_mate[k] = send(hbuf.at[:, other, cols[k]], precv.at[k], ps.at[k], pr.at[k], mate)

    def chip_sum(k):
        to_mate[k].wait_recv()
        for i in range(2):
            both = hbuf[i, mine, cols[k]] + precv[k, i]
            hbuf[i, mine, cols[k]] = both
            xsend[k, i] = both.astype(BF16)
        to_chips[k] = [
            send(xsend.at[k], xrecv.at[o, k], xs.at[o, k], xr.at[o, k], device)
            for o, device in enumerate(across)
        ]

    def activate(k):
        hidden, hidden_tan = hbuf[0, mine, cols[k]], hbuf[1, mine, cols[k]]
        for o, copy in enumerate(to_chips[k]):
            copy.wait_recv()
            hidden = hidden + xrecv[o, k, 0].astype(F32)
            hidden_tan = hidden_tan + xrecv[o, k, 1].astype(F32)
        active, active_tan, slope = gelu_parts(hidden, hidden_tan)
        acts[0, mine, cols[k]] = active_tan.astype(BF16)
        acts[1, mine, cols[k]] = active.astype(BF16)
        slopes[:, cols[k]] = slope
        part = acts.at[:, mine, cols[k]]
        halves[k] = send(part, part, as_.at[k], ar.at[k], mate)

    scatter, gather = {}, {}

    def second(k, begin, last):
        for j in range(begin, k + 1):
            halves[j].wait_recv()
        w, base = begin // per, (begin % per) * cw
        span, here = (k + 1 - begin) * cw, pl.ds(begin * cw, (k + 1 - begin) * cw)
        for i in range(2):
            load(2 + i, w)
        for n in range(no):
            part = pl.ds(n * dn, dn)
            term = None
            for i in range(2):
                product = jnp.dot(
                    acts[i, :, here], w2[i, w, pl.ds(base, span), part], preferred_element_type=F32
                )
                term = product if term is None else term + product
            if begin > 0:
                term += acc[n]
            acc[n] = term
            if last:
                rsend[n] = term.reshape(group, tl, dn).astype(BF16)
                scatter[n] = [
                    send(rsend.at[n, r], rrecv.at[n, o], rs.at[n, o], rr.at[n, o], device)
                    for o, (r, device) in enumerate(zip(ranks, peers))
                ]

    for t in range(nf + LAG_CHIP):
        if t < nf:
            first(t)
        if t >= LAG_CHIP:
            chip_sum(t - LAG_CHIP)
    begin = 0
    for t in range(nf + LAG_SECOND):
        if t < nf:
            activate(t)
        k = t - LAG_SECOND
        if k >= 0 and ((k + 1) % per == 0 or k // per == nw - 1):
            second(k, begin, k == nf - 1)
            begin = k + 1
    act_out[...] = acts[1]

    for n in range(no):
        value = acc[n, pl.ds(pl.multiple_of(me * tl, tl), tl), :]
        for o, copy in enumerate(scatter[n]):
            copy.wait_recv()
            value += rrecv[n, o].astype(F32)
        outg[n, me] = value.astype(BF16)
        gather[n] = [
            send(outg.at[n, me], outg.at[n, me], gs.at[n, o], gr.at[n, o], device)
            for o, device in enumerate(peers)
        ]

    to_mate = {}
    wide = nf // GROUPS if nf % GROUPS == 0 else 1

    def back_chip_sum(g):
        to_mate[g].wait_recv()
        span = pl.ds(g * wide * cw, wide * cw)
        both = bbuf[mine, span] + brecv[g]
        sum_out[:, span] = both
        cross_out[:, span] = both.astype(BF16)

    for n in range(no):
        for copy in gather[n]:
            copy.wait_recv()
        part = pl.ds(n * dn, dn)
        tan2d[:, part] = outg[n].astype(F32).reshape(total, dn).astype(BF16)
        for k in range(nf):
            term = lax.dot_general(
                tan2d[:, part], w2[0, k // per, pl.ds((k % per) * cw, cw), part],
                (((1,), (1,)), ((), ())), preferred_element_type=F32,
            )
            if n > 0:
                term += bbuf[:, cols[k]]
            bbuf[:, cols[k]] = term
            if n == no - 1 and (k + 1) % wide == 0:
                g = k // wide
                span = pl.ds(g * wide * cw, wide * cw)
                to_mate[g] = send(bbuf.at[other, span], brecv.at[g], bps.at[g], bpr.at[g], mate)
    for g in range(nf // wide):
        back_chip_sum(g)
    for copy in sent:
        copy.wait_send()


def second_kernel(factor, act_ref, tan_ref, out_ref, buf, sem):
    n, step = buf.shape[:2]
    copies = []
    for j in range(n):
        part = pl.ds(j * step, step)
        buf[j] = factor * lax.dot_general(
            act_ref[:, part], tan_ref[...], (((0,), (0,)), ((), ())), preferred_element_type=F32
        )
        copy = pltpu.make_async_copy(buf.at[j], out_ref.at[part, :], sem.at[j])
        copy.start()
        copies.append(copy)
    for copy in copies:
        copy.wait()


def first_kernel(factor, tok_ref, own_ref, mate_ref, out_ref, both, buf, sem):
    n, step = buf.shape[:2]
    half = own_ref.shape[0]
    both[pl.ds(0, half), :] = own_ref[...]
    both[pl.ds(half, half), :] = mate_ref[...]
    copies = []
    for j in range(n):
        part = pl.ds(j * step, step)
        buf[j] = factor * lax.dot_general(
            tok_ref[:, part], both[...], (((0,), (0,)), ((), ())), preferred_element_type=F32
        )
        copy = pltpu.make_async_copy(buf.at[j], out_ref.at[part, :], sem.at[j])
        copy.start()
        copies.append(copy)
    for copy in copies:
        copy.wait()


def on_device(axes, tokens, first_weight, first_tangent, second_weight, second_tangent):
    tl, dl = tokens.shape
    fl = first_weight.shape[1]
    ncol, ndepth, chips = axes["col"], axes["depth"], axes["row"] // CORES
    group = ncol * ndepth
    total, half = group * tl, group * tl // CORES
    nw, no = pieces(fl, 6), pieces(dl, 3)
    nf = 2 * nw if (fl // nw) % (2 * LANES) == 0 else nw
    cw, ww, dn = fl // nf, fl // nw, dl // no
    far = max(chips - 1, 1)
    groups = GROUPS if nf % GROUPS == 0 else nf
    factor = 1.0 / math.sqrt(total)
    dma = pltpu.SemaphoreType.DMA
    hbm = pl.BlockSpec(memory_space=pl.ANY)
    vmem = pl.BlockSpec(memory_space=pltpu.VMEM)
    gathered, active, out_tan, cross, own_sum, slopes = pl.pallas_call(
        functools.partial(block_kernel, (chips, ncol, ndepth, nw, nf, no)),
        name="block",
        out_shape=(
            jax.ShapeDtypeStruct((total, dl), BF16),
            jax.ShapeDtypeStruct((total, fl), BF16),
            jax.ShapeDtypeStruct((total, dl), BF16),
            jax.ShapeDtypeStruct((half, fl), BF16),
            jax.ShapeDtypeStruct((half, fl), F32),
            jax.ShapeDtypeStruct((half, fl), F32),
        ),
        in_specs=[hbm] * 5,
        out_specs=(vmem,) * 6,
        scratch_shapes=[
            pltpu.VMEM((2, nw, dl, ww), BF16),
            pltpu.VMEM((2, nw, ww, dl), BF16),
            pltpu.VMEM((group, tl, dl), BF16),
            pltpu.VMEM((total, dl), BF16),
            pltpu.VMEM((2, total, fl), F32),
            pltpu.VMEM((nf, 2, half, cw), F32),
            pltpu.VMEM((nf, 2, half, cw), BF16),
            pltpu.VMEM((far, nf, 2, half, cw), BF16),
            pltpu.VMEM((2, total, fl), BF16),
            pltpu.VMEM((no, total, dn), F32),
            pltpu.VMEM((no, group, tl, dn), BF16),
            pltpu.VMEM((no, group - 1, tl, dn), BF16),
            pltpu.VMEM((no, group, tl, dn), BF16),
            pltpu.VMEM((total, fl), F32),
            pltpu.VMEM((groups, half, fl // groups), F32),
            dma((4, nw)),
            dma,
            dma((group - 1,)), dma((group - 1,)),
            dma((nf,)), dma((nf,)),
            dma((far, nf)), dma((far, nf)),
            dma((nf,)), dma((nf,)),
            dma((no, group - 1)), dma((no, group - 1)),
            dma((no, group - 1)), dma((no, group - 1)),
            dma((groups,)), dma((groups,)),
        ],
        compiler_params=pltpu.CompilerParams(
            collective_id=0, has_side_effects=True, vmem_limit_bytes=VMEM_MIB * 1024 * 1024
        ),
    )(tokens, first_weight, first_tangent, second_weight, second_tangent)

    rows = range(chips * CORES)
    value = own_sum
    arrived = [
        lax.ppermute(cross, "row", [(r, (r + o * CORES) % (chips * CORES)) for r in rows])
        for o in range(1, chips)
    ]
    ns, nd = pieces(fl, STEPS), pieces(dl, STEPS)
    cost = pl.CostEstimate(flops=2 * total * fl * dl, bytes_accessed=4 * fl * dl, transcendentals=0)
    params = pltpu.CompilerParams(vmem_limit_bytes=GRADS_MIB * 1024 * 1024)
    grad_second = pl.pallas_call(
        functools.partial(second_kernel, factor),
        name="second",
        out_shape=jax.ShapeDtypeStruct((fl, dl), F32),
        in_specs=[vmem] * 2,
        out_specs=hbm,
        scratch_shapes=[pltpu.VMEM((ns, fl // ns, dl), F32), dma((ns,))],
        cost_estimate=cost,
        compiler_params=params,
    )(active, out_tan)
    arrived, grad_second = lax.optimization_barrier((arrived, grad_second))
    for part in arrived:
        value = value + part.astype(F32)
    back = (value * slopes).astype(BF16)
    other = lax.ppermute(back, "row", [(r, r + 1 - 2 * (r % CORES)) for r in rows])
    grad_first = pl.pallas_call(
        functools.partial(first_kernel, factor),
        name="first",
        out_shape=jax.ShapeDtypeStruct((dl, fl), F32),
        in_specs=[vmem] * 3,
        out_specs=hbm,
        scratch_shapes=[
            pltpu.VMEM((total, fl), BF16), pltpu.VMEM((nd, dl // nd, fl), F32), dma((nd,))
        ],
        cost_estimate=cost,
        compiler_params=params,
    )(gathered, back, other)
    return grad_first, grad_second


def solution(mesh):
    return jax.shard_map(
        functools.partial(on_device, dict(mesh.shape)),
        mesh=mesh,
        in_specs=(
            P(("col", "depth"), "row"),
            P("row", ("col", "depth")),
            P("row", ("col", "depth")),
            P(("col", "depth"), "row"),
            P(("col", "depth"), "row"),
        ),
        out_specs=(P("row", ("col", "depth")), P(("col", "depth"), "row")),
        check_vma=False,
    )
```

time: 64.6 us -> 58.2 us (0.901)
  Pallas kernels: 63.8 us -> 54.5 us
  waiting for transfers between devices: 0 us -> 1.2 us
  starting transfers between devices: 0 us -> 0.92 us
  local copies, waits for them, and re-layouts: 0 us -> 0.73 us
    pallas_call x2 -> x3, Pallas kernels: 63.8 us -> 54.5 us  [the longest x1 40.5 us: on_device(): pl.pallas_call(functools.partial(block_kernel, (chips, ncol, ndepth, nw,...]
    ppermute x0 -> x2, waiting for transfers between devices: none -> 1.2 us  [the longest x1 1.19 us: on_device(): lax.ppermute(back, 'row', [(r, r + 1 - 2 * (r % CORES)) for r in rows])]
    ppermute x0 -> x2, starting transfers between devices: none -> 0.92 us  [the longest x1 0.6 us: on_device(): lax.ppermute(cross, 'row', [(r, (r + o * CORES) % (chips * CORES)) for r...]
    unnamed x0 -> x2, local copies, waits for them, and re-layouts: none -> 0.73 us
  transfers between devices with their start and end apart: 0 -> 2, of which waited for: 0 -> 1; matrix products, arithmetic and copies ran while one was open for 0% -> 0% of each run, Pallas kernels for 0% -> 12%
where the time goes in v1:
time: 58.2 us; the launch traced here: 58 us
  Pallas kernels  54.5 us (94%)
  waiting for transfers between devices  1.2 us (2%)
  starting transfers between devices  0.92 us (2%)
  local copies, waits for them, and re-layouts  0.73 us (1%)
  between operations  0.67 us (1%)
    pallas_call x1, Pallas kernels, on_device(): pl.pallas_call(functools.partial(block_kernel, (chips, ncol, ndepth, nw,...  40.5 us
    pallas_call x1, Pallas kernels, on_device(): pl.pallas_call(functools.partial(first_kernel, factor), name='first', out...  6.98 us
    pallas_call x1, Pallas kernels, on_device(): pl.pallas_call(functools.partial(second_kernel, factor), name='second', o...  6.97 us
    ppermute x1, waiting for transfers between devices, on_device(): lax.ppermute(back, 'row', [(r, r + 1 - 2 * (r % CORES)) for r in rows])  1.19 us
  transfers between devices with their start and end apart: 2, of which 1 were waited for; matrix products, arithmetic and copies ran while one was open for 0% of the time, Pallas kernels for 12%

profile of v1, /device:TPU:0, one launch (start us, length us, event | category | flops | bytes accessed | tf_op | source)
XLA Modules:
  0.0 58.0 jit_solution(12456333507656895384)
XLA Ops:
  0.6 0.0 copy-start
  0.6 0.7 %copy-done = bf16[8,1536]{1,0:T(8,128)(2,1)S(1)} copy-done((bf16[8,1536]{1,0:T(8,128)(2,1)S(1)}, bf16[8,1536]{1,0:T(8,128)(2,1)}, u32[]{:S(2)}) %copy-start) | copy-done | bytes 24600
  1.4 40.5 %block.1 = (bf16[64,1536]{1,0:T(8,128)(2,1)S(1)}, bf16[64,3072]{1,0:T(8,128)(2,1)S(1)}, bf16[64,1536]{1,0:T(8,128)(2,1)S(1)}, bf16[32,3072]{1,0:T(8,128)(2,1)S(1...) custom-call(bf16[8,1536]{1,0:T(8,128)(2,1)S(1)} %copy-done, bf16[1536,3072]{1,0:T(8,128)(2,1)} %fw_ref.1, ...), custom_call_target="tpu_custom_call" | custom-call | tf_op jit(solution)/shard_map/block/pallas_call | solution.py:290
  41.9 0.6 %collective-permute-start = (bf16[32,3072]{1,0:T(8,128)(2,1)S(1)}, bf16[32,3072]{1,0:T(8,128)(2,1)S(1)}, u32[]{:S(2)}, u32[]{:S(2)}) collective-permute-start(bf16[32,3072]{1,0:T(8,128)(2,1)S(1)} %get-tuple-element.12), channel_id=1, source_target_pairs={{0,16},{8,24},{16,0},{24,8},{1,17},{9,25},{17,1},{25,9},{2,18},{10... | collective-permute-start | bytes 589832 | tf_op jit(solution)/shard_map/ppermute | solution.py:337
  42.5 7.0 %second.1 = f32[3072,1536]{1,0:T(8,128)} custom-call(bf16[64,3072]{1,0:T(8,128)(2,1)S(1)} %get-tuple-element.13.act_ref, bf16[64,1536]{1,0:T(8,128)(2,1)S(1)} %get-tuple-element.14.tan_ref), custom_call_target="tpu_custom_call" | custom-call | flops 603979776 | bytes 18874368 | tf_op jit(solution)/shard_map/second/pallas_call | solution.py:343
  49.5 0.0 collective-permute-done
  49.5 0.1 multiply_convert_fusion.own_ref
  49.5 0.3 collective-permute-start.1
  49.9 1.2 %collective-permute-done.1.mate_ref = bf16[32,3072]{1,0:T(8,128)(2,1)S(1)} collective-permute-done((bf16[32,3072]{1,0:T(8,128)(2,1)S(1)}, bf16[32,3072]{1,0:T(8,128)(2,1)S(1)}, u32[]{:S(2)}, u32[]{:S(2)}) %collective-permute-start.1) | collective-permute-done | bytes 196640 | tf_op jit(solution)/shard_map/ppermute | solution.py:357
  51.1 7.0 %first.1 = f32[1536,3072]{1,0:T(8,128)} custom-call(bf16[64,1536]{1,0:T(8,128)(2,1)S(1)} %get-tuple-element.10.tok_ref, bf16[32,3072]{1,0:T(8,128)(2,1)S(1)} %multiply_convert_fusion.own_ref, bf16[32,3072]{1,0:T(8,128)(2,1)S(1)} %collective-permute-done.1.mate_ref), custom_call_target="tpu_custom_call" | custom-call | flops 603979776 | bytes 18874368 | tf_op jit(solution)/shard_map/first/pallas_call | solution.py:358
Async XLA Ops:
  0.6 0.7 %copy-start = (bf16[8,1536]{1,0:T(8,128)(2,1)S(1)}, bf16[8,1536]{1,0:T(8,128)(2,1)}, u32[]{:S(2)}) copy-start(bf16[8,1536]{1,0:T(8,128)(2,1)} %tok_ref.1) | copy-start | bytes 73732
  41.9 7.6 %collective-permute-start = (bf16[32,3072]{1,0:T(8,128)(2,1)S(1)}, bf16[32,3072]{1,0:T(8,128)(2,1)S(1)}, u32[]{:S(2)}, u32[]{:S(2)}) collective-permute-start(bf16[32,3072]{1,0:T(8,128)(2,1)S(1)} %get-tuple-element.12), channel_id=1, source_target_pairs={{0,16},{8,24},{16,0},{24,8},{1,17},{9,25},{17,1},{25,9},{2,18},{10... | collective-permute-start | bytes 589832 | tf_op jit(solution)/shard_map/ppermute | solution.py:337
  49.5 1.5 %collective-permute-start.1 = (bf16[32,3072]{1,0:T(8,128)(2,1)S(1)}, bf16[32,3072]{1,0:T(8,128)(2,1)S(1)}, u32[]{:S(2)}, u32[]{:S(2)}) collective-permute-start(bf16[32,3072]{1,0:T(8,128)(2,1)S(1)} %multiply_convert_fusion.own_ref), channel_id=1, source_target_pairs={{0,8},{8,0},{16,24},{24,16},{1,9},{9,1},{17,25},{25,17},{2,10},{10... | collective-permute-start | bytes 589832 | tf_op jit(solution)/shard_map/ppermute | solution.py:357

commit v2 on v1

--- a/solution.py
+++ b/solution.py
@@ -72,44 +72,34 @@
     for i, ref in enumerate((fw_ref, ft_ref)):
         for k in range(nw):
             loads[i, k] = pltpu.make_async_copy(
-                ref.at[:, pl.ds(k * ww, ww)], w1.at[i, k], wsem.at[i, k]
+                ref.at[:, pl.ds(k * ww, ww)], w1.at[i, k], wsem.at[0]
             )
     for i, ref in enumerate((sw_ref, st_ref)):
         for k in range(nw):
             loads[2 + i, k] = pltpu.make_async_copy(
-                ref.at[pl.ds(k * ww, ww), :], w2.at[i, k], wsem.at[2 + i, k]
+                ref.at[pl.ds(k * ww, ww), :], w2.at[i, k], wsem.at[1]
             )
     for pair in (0, 2):
         for k in range(nw):
             loads[pair, k].start()
             loads[pair + 1, k].start()
-    loaded = set()
-
-    def load(i, k):
-        if (i, k) not in loaded:
-            loaded.add((i, k))
-            loads[i, k].wait()
-
-    sent = []
-
     def send(src, dst, ssem, rsem, device):
         copy = pltpu.make_async_remote_copy(
             src_ref=src, dst_ref=dst, send_sem=ssem, recv_sem=rsem,
             device_id=device, device_id_type=pl.DeviceIdType.MESH,
         )
         copy.start()
-        sent.append(copy)
         return copy
+
+    def all_of(ref, sem):
+        pltpu.make_async_copy(ref, ref, sem).wait()
 
     own.wait()
     pl.semaphore_wait(barrier, len(entry))
 
-    arrivals = [
-        send(tokg.at[me], tokg.at[me], tok_s.at[o], tok_r.at[o], device)
-        for o, device in enumerate(peers)
-    ]
-    for copy in arrivals:
-        copy.wait_recv()
+    for device in peers:
+        send(tokg.at[me], tokg.at[me], tok_s, tok_r, device)
+    all_of(tokg.at[pl.ds(0, group - 1)], tok_r)
     tok2d[...] = tokg[...].astype(F32).reshape(total, dl).astype(BF16)
 
     tok_out[pl.ds(0, half), :] = tok2d[mine, :]
@@ -119,15 +109,13 @@
     to_mate, to_chips, halves = {}, {}, {}
     per = nf // nw
 
-    for i in range(2):
-        for k in range(nw):
-            load(i, k)
+    all_of(w1, wsem.at[0])
 
     def first(k):
         for i in range(2):
             weight = w1[i, k // per, :, pl.ds((k % per) * cw, cw)]
             hbuf[i, :, cols[k]] = jnp.dot(tok2d[...], weight, preferred_element_type=F32)
-        to_mate[k] = send(hbuf.at[:, other, cols[k]], precv.at[k], ps.at[k], pr.at[k], mate)
+        to_mate[k] = send(hbuf.at[:, other, cols[k]], precv.at[k], ps, pr.at[k], mate)
 
     def chip_sum(k):
         to_mate[k].wait_recv()
@@ -136,7 +124,7 @@
             hbuf[i, mine, cols[k]] = both
             xsend[k, i] = both.astype(BF16)
         to_chips[k] = [
-            send(xsend.at[k], xrecv.at[o, k], xs.at[o, k], xr.at[o, k], device)
+            send(xsend.at[k], xrecv.at[o, k], xs, xr.at[o, k], device)
             for o, device in enumerate(across)
         ]
 
@@ -151,17 +139,15 @@
         acts[1, mine, cols[k]] = active.astype(BF16)
         slopes[:, cols[k]] = slope
         part = acts.at[:, mine, cols[k]]
-        halves[k] = send(part, part, as_.at[k], ar.at[k], mate)
-
-    scatter, gather = {}, {}
+        halves[k] = send(part, part, as_, ar.at[k], mate)
 
     def second(k, begin, last):
         for j in range(begin, k + 1):
             halves[j].wait_recv()
         w, base = begin // per, (begin % per) * cw
         span, here = (k + 1 - begin) * cw, pl.ds(begin * cw, (k + 1 - begin) * cw)
-        for i in range(2):
-            load(2 + i, w)
+        if begin == 0:
+            all_of(w2, wsem.at[1])
         for n in range(no):
             part = pl.ds(n * dn, dn)
             term = None
@@ -175,10 +161,8 @@
             acc[n] = term
             if last:
                 rsend[n] = term.reshape(group, tl, dn).astype(BF16)
-                scatter[n] = [
-                    send(rsend.at[n, r], rrecv.at[n, o], rs.at[n, o], rr.at[n, o], device)
-                    for o, (r, device) in enumerate(zip(ranks, peers))
-                ]
+                for o, (r, device) in enumerate(zip(ranks, peers)):
+                    send(rsend.at[n, r], rrecv.at[n, o], rs, rr.at[n], device)
 
     for t in range(nf + LAG_CHIP):
         if t < nf:
@@ -197,14 +181,12 @@
 
     for n in range(no):
         value = acc[n, pl.ds(pl.multiple_of(me * tl, tl), tl), :]
-        for o, copy in enumerate(scatter[n]):
-            copy.wait_recv()
+        all_of(rrecv.at[n], rr.at[n])
+        for o in range(group - 1):
             value += rrecv[n, o].astype(F32)
         outg[n, me] = value.astype(BF16)
-        gather[n] = [
-            send(outg.at[n, me], outg.at[n, me], gs.at[n, o], gr.at[n, o], device)
-            for o, device in enumerate(peers)
-        ]
+        for device in peers:
+            send(outg.at[n, me], outg.at[n, me], gs, gr.at[n], device)
 
     to_mate = {}
     wide = nf // GROUPS if nf % GROUPS == 0 else 1
@@ -217,8 +199,7 @@
         cross_out[:, span] = both.astype(BF16)
 
     for n in range(no):
-        for copy in gather[n]:
-            copy.wait_recv()
+        all_of(outg.at[n, pl.ds(0, group - 1)], gr.at[n])
         part = pl.ds(n * dn, dn)
         tan2d[:, part] = outg[n].astype(F32).reshape(total, dn).astype(BF16)
         for k in range(nf):
@@ -232,11 +213,16 @@
             if n == no - 1 and (k + 1) % wide == 0:
                 g = k // wide
                 span = pl.ds(g * wide * cw, wide * cw)
-                to_mate[g] = send(bbuf.at[other, span], brecv.at[g], bps.at[g], bpr.at[g], mate)
+                to_mate[g] = send(bbuf.at[other, span], brecv.at[g], bps, bpr.at[g], mate)
     for g in range(nf // wide):
         back_chip_sum(g)
-    for copy in sent:
-        copy.wait_send()
+    all_of(tokg.at[pl.ds(0, group - 1)], tok_s)
+    all_of(precv, ps)
+    all_of(xrecv, xs)
+    all_of(acts.at[:, mine, :], as_)
+    all_of(rrecv, rs)
+    all_of(outg.at[:, pl.ds(0, group - 1)], gs)
+    all_of(brecv, bps)
 
 
 def second_kernel(factor, act_ref, tan_ref, out_ref, buf, sem):
@@ -316,20 +302,23 @@
             pltpu.VMEM((no, group, tl, dn), BF16),
             pltpu.VMEM((total, fl), F32),
             pltpu.VMEM((groups, half, fl // groups), F32),
-            dma((4, nw)),
+            dma((2,)),
             dma,
-            dma((group - 1,)), dma((group - 1,)),
-            dma((nf,)), dma((nf,)),
-            dma((far, nf)), dma((far, nf)),
-            dma((nf,)), dma((nf,)),
-            dma((no, group - 1)), dma((no, group - 1)),
-            dma((no, group - 1)), dma((no, group - 1)),
-            dma((groups,)), dma((groups,)),
+            dma, dma,
+            dma, dma((nf,)),
+            dma, dma((far, nf)),
+            dma, dma((nf,)),
+            dma, dma((no,)),
+            dma, dma((no,)),
+            dma, dma((groups,)),
         ],
         compiler_params=pltpu.CompilerParams(
             collective_id=0, has_side_effects=True, vmem_limit_bytes=VMEM_MIB * 1024 * 1024
         ),
-    )(tokens, first_weight, first_tangent, second_weight, second_tangent)
+    )(
+        pltpu.with_memory_space_constraint(tokens, pltpu.HBM),
+        first_weight, first_tangent, second_weight, second_tangent,
+    )
 
     rows = range(chips * CORES)
     value = own_sum

time: 58.2 us -> 66.4 us (1.14)
  Pallas kernels: 54.5 us -> 63.4 us
  local copies, waits for them, and re-layouts: 0.73 us -> 0 us
    pallas_call x1, Pallas kernels: 40.5 us -> 49.5 us  [on_device(): pl.pallas_call(functools.partial(block_kernel, (chips, ncol, ndepth, nw,...]
    unnamed x2 -> x0, local copies, waits for them, and re-layouts: 0.73 us -> none
  transfers between devices with their start and end apart: 2 -> 2, of which waited for: 1 -> 1; matrix products, arithmetic and copies ran while one was open for 0% -> 0% of each run, Pallas kernels for 12% -> 11%
where the time goes in v2:
time: 66.4 us; the launch traced here: 66.2 us
  Pallas kernels  63.4 us (95%)
  waiting for transfers between devices  1.32 us (2%)
  starting transfers between devices  0.79 us (1%)
    pallas_call x1, Pallas kernels, on_device(): pl.pallas_call(functools.partial(block_kernel, (chips, ncol, ndepth, nw,...  49.5 us
    pallas_call x1, Pallas kernels, on_device(): pl.pallas_call(functools.partial(first_kernel, factor), name='first', out...  6.97 us
    pallas_call x1, Pallas kernels, on_device(): pl.pallas_call(functools.partial(second_kernel, factor), name='second', o...  6.97 us
  transfers between devices with their start and end apart: 2, of which 1 were waited for; matrix products, arithmetic and copies ran while one was open for 0% of the time, Pallas kernels for 11%

profile of v2, /device:TPU:0, one launch (start us, length us, event | category | flops | bytes accessed | tf_op | source)
XLA Modules:
  0.0 66.2 jit_solution(12358665899172485236)
XLA Ops:
  0.6 49.5 %block.1 = (bf16[64,1536]{1,0:T(8,128)(2,1)S(1)}, bf16[64,3072]{1,0:T(8,128)(2,1)S(1)}, bf16[64,1536]{1,0:T(8,128)(2,1)S(1)}, bf16[32,3072]{1,0:T(8,128)(2,1)S(1...) custom-call(bf16[8,1536]{1,0:T(8,128)(2,1)} %tok_ref.1, bf16[1536,3072]{1,0:T(8,128)(2,1)} %fw_ref.1, ...), custom_call_target="tpu_custom_call" | custom-call | tf_op jit(solution)/shard_map/block/pallas_call | solution.py:276
  50.1 0.6 collective-permute-start
  50.7 7.0 %second.1 = f32[3072,1536]{1,0:T(8,128)} custom-call(bf16[64,3072]{1,0:T(8,128)(2,1)S(1)} %get-tuple-element.13.act_ref, bf16[64,1536]{1,0:T(8,128)(2,1)S(1)} %get-tuple-element.14.tan_ref), custom_call_target="tpu_custom_call" | custom-call | flops 603979776 | bytes 18874368 | tf_op jit(solution)/shard_map/second/pallas_call | solution.py:332
  57.7 0.0 collective-permute-done
  57.7 0.1 multiply_convert_fusion.own_ref
  57.8 0.2 collective-permute-start.1
  57.9 1.3 %collective-permute-done.1.mate_ref = bf16[32,3072]{1,0:T(8,128)(2,1)S(1)} collective-permute-done((bf16[32,3072]{1,0:T(8,128)(2,1)S(1)}, bf16[32,3072]{1,0:T(8,128)(2,1)S(1)}, u32[]{:S(2)}, u32[]{:S(2)}) %collective-permute-start.1) | collective-permute-done | bytes 196640 | tf_op jit(solution)/shard_map/ppermute | solution.py:346
  59.3 7.0 %first.1 = f32[1536,3072]{1,0:T(8,128)} custom-call(bf16[64,1536]{1,0:T(8,128)(2,1)S(1)} %get-tuple-element.10.tok_ref, bf16[32,3072]{1,0:T(8,128)(2,1)S(1)} %multiply_convert_fusion.own_ref, bf16[32,3072]{1,0:T(8,128)(2,1)S(1)} %collective-permute-done.1.mate_ref), custom_call_target="tpu_custom_call" | custom-call | flops 603979776 | bytes 18874368 | tf_op jit(solution)/shard_map/first/pallas_call | solution.py:347
Async XLA Ops:
  50.1 7.6 %collective-permute-start = (bf16[32,3072]{1,0:T(8,128)(2,1)S(1)}, bf16[32,3072]{1,0:T(8,128)(2,1)S(1)}, u32[]{:S(2)}, u32[]{:S(2)}) collective-permute-start(bf16[32,3072]{1,0:T(8,128)(2,1)S(1)} %get-tuple-element.12), channel_id=1, source_target_pairs={{0,16},{8,24},{16,0},{24,8},{1,17},{9,25},{17,1},{25,9},{2,18},{10... | collective-permute-start | bytes 589832 | tf_op jit(solution)/shard_map/ppermute | solution.py:326
  57.8 1.5 %collective-permute-start.1 = (bf16[32,3072]{1,0:T(8,128)(2,1)S(1)}, bf16[32,3072]{1,0:T(8,128)(2,1)S(1)}, u32[]{:S(2)}, u32[]{:S(2)}) collective-permute-start(bf16[32,3072]{1,0:T(8,128)(2,1)S(1)} %multiply_convert_fusion.own_ref), channel_id=1, source_target_pairs={{0,8},{8,0},{16,24},{24,16},{1,9},{9,1},{17,25},{25,17},{2,10},{10... | collective-permute-start | bytes 589832 | tf_op jit(solution)/shard_map/ppermute | solution.py:346

commit v3 on v2

--- a/solution.py
+++ b/solution.py
@@ -68,6 +68,7 @@
 
     own = pltpu.make_async_copy(tok_ref, tokg.at[me], own_s)
     own.start()
+    own.wait()
     loads = {}
     for i, ref in enumerate((fw_ref, ft_ref)):
         for k in range(nw):
@@ -94,7 +95,6 @@
     def all_of(ref, sem):
         pltpu.make_async_copy(ref, ref, sem).wait()
 
-    own.wait()
     pl.semaphore_wait(barrier, len(entry))
 
     for device in peers:

time: 66.4 us -> 56.2 us (0.85)
  Pallas kernels: 63.4 us -> 53.1 us
    pallas_call x1, Pallas kernels: 49.5 us -> 39.2 us  [on_device(): pl.pallas_call(functools.partial(block_kernel, (chips, ncol, ndepth, nw,...]
  transfers between devices with their start and end apart: 2 -> 2, of which waited for: 1 -> 1; matrix products, arithmetic and copies ran while one was open for 0% -> 0% of each run, Pallas kernels for 11% -> 12%
where the time goes in v3:
time: 56.2 us; the launch traced here: 56.1 us
  Pallas kernels  53.1 us (94%)
  waiting for transfers between devices  1.32 us (2%)
  starting transfers between devices  0.88 us (2%)
  between operations  0.66 us (1%)
    pallas_call x1, Pallas kernels, on_device(): pl.pallas_call(functools.partial(block_kernel, (chips, ncol, ndepth, nw,...  39.2 us
    pallas_call x1, Pallas kernels, on_device(): pl.pallas_call(functools.partial(first_kernel, factor), name='first', out...  6.97 us
    pallas_call x1, Pallas kernels, on_device(): pl.pallas_call(functools.partial(second_kernel, factor), name='second', o...  6.97 us
    ppermute x1, waiting for transfers between devices, on_device(): lax.ppermute(back, 'row', [(r, r + 1 - 2 * (r % CORES)) for r in rows])  1.32 us
  transfers between devices with their start and end apart: 2, of which 1 were waited for; matrix products, arithmetic and copies ran while one was open for 0% of the time, Pallas kernels for 12%

profile of v3, /device:TPU:0, one launch (start us, length us, event | category | flops | bytes accessed | tf_op | source)
XLA Modules:
  0.0 56.1 jit_solution(8116719163220833480)
XLA Ops:
  0.6 39.2 %block.1 = (bf16[64,1536]{1,0:T(8,128)(2,1)S(1)}, bf16[64,3072]{1,0:T(8,128)(2,1)S(1)}, bf16[64,1536]{1,0:T(8,128)(2,1)S(1)}, bf16[32,3072]{1,0:T(8,128)(2,1)S(1...) custom-call(bf16[8,1536]{1,0:T(8,128)(2,1)} %tok_ref.1, bf16[1536,3072]{1,0:T(8,128)(2,1)} %fw_ref.1, ...), custom_call_target="tpu_custom_call" | custom-call | tf_op jit(solution)/shard_map/block/pallas_call | solution.py:276
  39.8 0.7 %collective-permute-start = (bf16[32,3072]{1,0:T(8,128)(2,1)S(1)}, bf16[32,3072]{1,0:T(8,128)(2,1)S(1)}, u32[]{:S(2)}, u32[]{:S(2)}) collective-permute-start(bf16[32,3072]{1,0:T(8,128)(2,1)S(1)} %get-tuple-element.12), channel_id=1, source_target_pairs={{0,16},{8,24},{16,0},{24,8},{1,17},{9,25},{17,1},{25,9},{2,18},{10... | collective-permute-start | bytes 589832 | tf_op jit(solution)/shard_map/ppermute | solution.py:326
  40.5 7.0 %second.1 = f32[3072,1536]{1,0:T(8,128)} custom-call(bf16[64,3072]{1,0:T(8,128)(2,1)S(1)} %get-tuple-element.13.act_ref, bf16[64,1536]{1,0:T(8,128)(2,1)S(1)} %get-tuple-element.14.tan_ref), custom_call_target="tpu_custom_call" | custom-call | flops 603979776 | bytes 18874368 | tf_op jit(solution)/shard_map/second/pallas_call | solution.py:332
  47.5 0.0 collective-permute-done
  47.5 0.1 multiply_convert_fusion.own_ref
  47.6 0.2 collective-permute-start.1
  47.8 1.3 %collective-permute-done.1.mate_ref = bf16[32,3072]{1,0:T(8,128)(2,1)S(1)} collective-permute-done((bf16[32,3072]{1,0:T(8,128)(2,1)S(1)}, bf16[32,3072]{1,0:T(8,128)(2,1)S(1)}, u32[]{:S(2)}, u32[]{:S(2)}) %collective-permute-start.1) | collective-permute-done | bytes 196640 | tf_op jit(solution)/shard_map/ppermute | solution.py:346
  49.1 7.0 %first.1 = f32[1536,3072]{1,0:T(8,128)} custom-call(bf16[64,1536]{1,0:T(8,128)(2,1)S(1)} %get-tuple-element.10.tok_ref, bf16[32,3072]{1,0:T(8,128)(2,1)S(1)} %multiply_convert_fusion.own_ref, bf16[32,3072]{1,0:T(8,128)(2,1)S(1)} %collective-permute-done.1.mate_ref), custom_call_target="tpu_custom_call" | custom-call | flops 603979776 | bytes 18874368 | tf_op jit(solution)/shard_map/first/pallas_call | solution.py:347
Async XLA Ops:
  39.8 7.7 %collective-permute-start = (bf16[32,3072]{1,0:T(8,128)(2,1)S(1)}, bf16[32,3072]{1,0:T(8,128)(2,1)S(1)}, u32[]{:S(2)}, u32[]{:S(2)}) collective-permute-start(bf16[32,3072]{1,0:T(8,128)(2,1)S(1)} %get-tuple-element.12), channel_id=1, source_target_pairs={{0,16},{8,24},{16,0},{24,8},{1,17},{9,25},{17,1},{25,9},{2,18},{10... | collective-permute-start | bytes 589832 | tf_op jit(solution)/shard_map/ppermute | solution.py:326
  47.6 1.5 %collective-permute-start.1 = (bf16[32,3072]{1,0:T(8,128)(2,1)S(1)}, bf16[32,3072]{1,0:T(8,128)(2,1)S(1)}, u32[]{:S(2)}, u32[]{:S(2)}) collective-permute-start(bf16[32,3072]{1,0:T(8,128)(2,1)S(1)} %multiply_convert_fusion.own_ref), channel_id=1, source_target_pairs={{0,8},{8,0},{16,24},{24,16},{1,9},{9,1},{17,25},{25,17},{2,10},{10... | collective-permute-start | bytes 589832 | tf_op jit(solution)/shard_map/ppermute | solution.py:346
